TPU v7x, 32 devices: a whole 2x2x4 slice. The times are simulated.
32 devices in a mesh: rows: 16 (over z, y, x), grid: 2 (over core).
Axes of the slice: x: 2, y: 2, z: 4, core: 2. Of those that a mesh axis runs over, the one named last changes fastest.
Arguments:
- library: bfloat16 [8192, 4096], P('rows', 'grid'), may hold values from -6 to 6
- col_scale: float32 [4096], replicated, may hold values from 0.5 to 2
Outputs:
- updated: float32 [4096, 4096], P('rows', 'grid')
- reflectors: float32 [4096, 64], P('rows')
All inputs are finite; a program needn't handle non-finite values.
Results may differ from a plain program's by a relative error of at most 0.0003.
Values may be sent and summed in bfloat16 or wider, within the bound.
A program may use at most 128 MiB of HBM per device.

v0:
```python
import jax
import jax.numpy as jnp
from jax import lax
from jax.sharding import PartitionSpec as P

PANEL = 64


def broadcast(block, axis, source):
    block = jnp.where(lax.axis_index(axis) == source, block, jnp.zeros_like(block))
    return lax.psum(block, axis)


def reflect_panel(panel):
    size, width = panel.shape
    row_line = jnp.arange(size)
    col_line = jnp.arange(width)
    vectors = jnp.zeros((size, width), jnp.float32)
    factor = jnp.zeros((width, width), jnp.float32)

    def one_step(step, carry):
        work, vectors, factor = carry
        column = jnp.sum(jnp.where(col_line[None, :] == step, work, 0.0), axis=1)
        column = jnp.where(row_line >= step, column, 0.0)
        pivot = jnp.sum(jnp.where(row_line == step, column, 0.0))
        length = jnp.sqrt(jnp.sum(column * column))
        sign_factor = jnp.where(pivot >= 0.0, 1.0, -1.0)
        vector = column + jnp.where(row_line == step, sign_factor * length, 0.0)
        scale = 2.0 / jnp.sum(vector * vector)
        project = jnp.dot(vector, work, precision=lax.Precision.HIGHEST)
        work = work - scale * vector[:, None] * project[None, :]
        coupling = jnp.dot(vector, vectors, precision=lax.Precision.HIGHEST)
        column_t = -scale * jnp.dot(factor, coupling, precision=lax.Precision.HIGHEST)
        column_t = column_t + jnp.where(col_line == step, scale, 0.0)
        factor = jnp.where(col_line[None, :] == step, column_t[:, None], factor)
        vectors = jnp.where(col_line[None, :] == step, vector[:, None], vectors)
        return (work, vectors, factor)

    work, vectors, factor = lax.fori_loop(0, width, one_step, (panel, vectors, factor))
    return (vectors, factor)


def per_device(library, col_scale):
    rows_dev, col_block = library.shape
    count_rows = lax.axis_size("rows")
    count_grid = lax.axis_size("grid")
    columns = col_block * count_grid
    row_block = columns // count_rows
    total = rows_dev * count_rows
    grid_place = lax.axis_index("grid")
    rows_place = lax.axis_index("rows")
    own_scale = lax.dynamic_slice_in_dim(col_scale, grid_place * col_block, col_block)
    whole = lax.all_gather(library, "grid", axis=1, tiled=True)
    product = lax.dot_general(
        whole, library, (((0,), (0,)), ((), ())), preferred_element_type=jnp.float32
    )
    gram = lax.psum_scatter(
        product * (col_scale[:, None] * own_scale[None, :] / total),
        "rows",
        scatter_dimension=0,
        tiled=True,
    )
    head = gram[:, :PANEL]
    head = broadcast(head, "grid", 0)
    panel = lax.all_gather(head, "rows", axis=0, tiled=True)
    vectors, factor = reflect_panel(panel)
    own_vectors = lax.dynamic_slice_in_dim(vectors, rows_place * row_block, row_block, 0)
    partial_cross = jnp.dot(own_vectors.T, gram, precision=lax.Precision.HIGHEST)
    cross = lax.psum(partial_cross, "rows")
    mixed = jnp.dot(factor.T, cross, precision=lax.Precision.HIGHEST)
    updated = gram - jnp.dot(own_vectors, mixed, precision=lax.Precision.HIGHEST)
    return (updated, own_vectors)


def solution(mesh):
    return jax.shard_map(
        per_device,
        mesh=mesh,
        in_specs=(P("rows", "grid"), P()),
        out_specs=(P("rows", "grid"), P("rows", None)),
        check_vma=False,
    )
```

profile of v0, /device:TPU:0, one launch (start us, length us, event | category | flops | bytes accessed | tf_op | source)
XLA Modules:
  0.0 1997.8 jit_solution(2636637013112608751)
XLA Ops:
  8.0 17.9 all-gather.3.cloned.1.call-done
  26.0 17.6 multiply_multiply_fusion
  43.7 684.7 %reduce-scatter.2.cloned.1.call-done = f32[256,2048]{1,0:T(8,128)} async-done(((f32[4096,2048]{1,0:T(8,128)}), f32[256,2048]{1,0:T(8,128)}) %reduce-scatter.2.cloned.1.call-update) | async-done | bytes 2097168 | tf_op jit(solution)/shard_map/reduce_scatter | solution.py:57
  730.0 24.8 %all-reduce.3.cloned.1.call-done = f32[256,64]{1,0:T(8,128)} async-done(((f32[256,64]{1,0:T(8,128)}), f32[256,64]{1,0:T(8,128)}) %all-reduce.3.cloned.1.call-update) | async-done | bytes 65552 | tf_op jit(solution)/shard_map/psum | solution.py:11
  755.2 64.3 %all-gather.5.cloned.1.call-done = f32[4096,64]{1,0:T(8,128)} async-done(((f32[256,64]{1,0:T(8,128)}), f32[4096,64]{1,0:T(8,128)}) %all-gather.5.cloned.1.call-update) | async-done | bytes 1048592 | tf_op jit(solution)/shard_map/all_gather | solution.py:65
  819.4 1055.3 %while.19 = (s32[]{:T(128)}, f32[4096,64]{1,0:T(8,128)}, f32[4096,64]{1,0:T(8,128)}, f32[64,64]{1,0:T(8,128)S(1)}, s32[]{:T(128)}, /*index=5*/f32[]{:T(128)}, f32[]{:T(128)}, f32[]{:T(128)}, f32[]{:T(128)}, s32[]{:T(128)}) while((s32[]{:T(128)}, f32[4096,64]{1,0:T(8,128)}, f32[4096,64]{1,0:T(8,128)}, ...), condition=%wide.region_7.8_spmd.clone.clone, body=%wide.region_2.7_spmd.clone.clone.sunk | while | flops 8245573 | bytes 24332360 | solution.py:39
  827.6 3.9 multiply_subtract_fusion.2
  844.1 3.9 multiply_subtract_fusion.2
  860.6 3.9 multiply_subtract_fusion.2
  877.2 3.9 multiply_subtract_fusion.2
  910.2 3.9 multiply_subtract_fusion.2
  926.7 3.9 multiply_subtract_fusion.2
  943.2 3.9 multiply_subtract_fusion.2
  959.7 3.9 multiply_subtract_fusion.2
  976.3 3.9 multiply_subtract_fusion.2
  992.8 3.9 multiply_subtract_fusion.2
  1009.3 3.9 multiply_subtract_fusion.2
  1025.8 3.9 multiply_subtract_fusion.2
  1042.3 3.9 multiply_subtract_fusion.2
  1058.8 3.9 multiply_subtract_fusion.2
  1075.4 3.9 multiply_subtract_fusion.2
  1091.9 3.9 multiply_subtract_fusion.2
  1108.4 3.9 multiply_subtract_fusion.2
  1124.9 3.9 multiply_subtract_fusion.2
  1141.4 3.9 multiply_subtract_fusion.2
  1157.9 3.9 multiply_subtract_fusion.2
  1174.5 3.9 multiply_subtract_fusion.2
  1191.0 3.9 multiply_subtract_fusion.2
  1224.0 3.9 multiply_subtract_fusion.2
  1240.5 3.9 multiply_subtract_fusion.2
  1257.0 3.9 multiply_subtract_fusion.2
  1879.3 107.1 %all-reduce.5.cloned.1.call-done = f32[64,2048]{1,0:T(8,128)} async-done(((f32[64,2048]{1,0:T(8,128)}), f32[64,2048]{1,0:T(8,128)}) %all-reduce.5.cloned.1.call-update) | async-done | bytes 524304 | tf_op jit(solution)/shard_map/psum | solution.py:69
  (1154 shorter events, 829.8 us)
Async XLA Ops:
  7.2 18.8 copy-start.5
  7.2 18.8 all-gather.3.cloned.1.call-start
  7.9 720.5 %reduce-scatter.2.cloned.1.call-start = ((), (), s32[]{:S(2)}) async-start(), calls=%async_computation.2 | async-start | bytes 35651584 | tf_op jit(solution)/shard_map/reduce_scatter | solution.py:57
  43.6 711.2 %all-reduce.3.cloned.1.call-start = ((), (), s32[]{:S(2)}) async-start(), calls=%async_computation.3 | async-start | bytes 262144 | tf_op jit(solution)/shard_map/psum | solution.py:11
  730.0 89.4 %all-gather.5.cloned.1.call-start = ((), (), s32[]{:S(2)}) async-start(), calls=%async_computation.4 | async-start | bytes 2228224 | tf_op jit(solution)/shard_map/all_gather | solution.py:65
  754.9 1231.5 %all-reduce.5.cloned.1.call-start = ((), (), s32[]{:S(2)}) async-start(), calls=%async_computation.5 | async-start | bytes 1048576 | tf_op jit(solution)/shard_map/psum | solution.py:69
  883.7 8.8 copy-start
  900.3 8.8 copy-start
  916.8 8.8 copy-start
  933.3 8.8 copy-start
  949.8 8.8 copy-start
  1048.9 8.8 copy-start
  1065.4 8.8 copy-start
  1082.0 8.8 copy-start
  1098.5 8.8 copy-start
  1197.6 8.8 copy-start
  1214.1 8.8 copy-start
  1230.6 8.8 copy-start
  1247.1 8.8 copy-start
  1263.6 8.8 copy-start
  1362.7 8.8 copy-start
  1379.3 8.8 copy-start
  1395.8 8.8 copy-start
  1412.3 8.8 copy-start
  1511.4 8.8 copy-start
  1527.9 8.8 copy-start
  1544.4 8.8 copy-start
  1560.9 8.8 copy-start
  1577.5 8.8 copy-start
  1676.6 8.8 copy-start
  1693.1 8.8 copy-start
  1877.1 111.0 %copy-start.6 = (f32[256,64]{0,1:T(8,128)}, f32[256,64]{0,1:T(8,128)S(1)}, u32[]{:S(2)}) copy-start(f32[256,64]{0,1:T(8,128)S(1)} %constant_dynamic-slice_fusion) | copy-start | bytes 196612
  (233 other events, 772.6 us)
Sparse Core Ops, SparseCore 0:
  9.6 16.3 all-gather.2
  43.8 684.5 reduce-scatter.1
  731.3 23.5 all-reduce.2
  757.5 61.8 all-gather.4
  1879.5 106.9 all-reduce.4
where the time goes:
time: 2000 us
  waiting for transfers between devices  900 us (45%)
  other arithmetic  496 us (25%)
  matrix products  290 us (14%)
  local copies, waits for them, and re-layouts  158 us (8%)
  loops' own time  140 us (7%)
    reduce_scatter x1, waiting for transfers between devices, per_device(): lax.psum_scatter(product * (col_scale[:, None] * own_scale[None, :] / tot...  685 us
    sub x64, other arithmetic, one_step(): work = work - scale * vector[:, None] * project[None, :]  250 us
    dot_general x64, matrix products, one_step(): coupling = jnp.dot(vector, vectors, precision=lax.Precision.HIGHEST)  184 us
    while x512, local copies, waits for them, and re-layouts  156 us
    reduce_sum x64, other arithmetic, one_step(): column = jnp.sum(jnp.where(col_line[None, :] == step, work, 0.0), axis=1)  150 us
    another operation x1, loops' own time, reflect_panel(): lax.fori_loop(0, width, one_step, (panel, vectors, factor))  140 us
    psum x1, waiting for transfers between devices, per_device(): cross = lax.psum(partial_cross, 'rows')  107 us
    dot_general x64, matrix products, one_step(): project = jnp.dot(vector, work, precision=lax.Precision.HIGHEST)  72.2 us
  transfers between devices with their start and end apart: 5, of which 5 were waited for; matrix products, arithmetic and copies ran while one was open for 0% of the time, Pallas kernels for 0%

commit v1 on v0

--- a/solution.py
+++ b/solution.py
@@ -62,7 +62,21 @@
     )
     head = gram[:, :PANEL]
     head = broadcast(head, "grid", 0)
-    panel = lax.all_gather(head, "rows", axis=0, tiled=True)
+    ways, here, turn = (lax.axis_size("rows"), lax.axis_index("rows"), head.shape[0])
+    shape = [n * ways if d == 0 else n for d, n in enumerate(head.shape)]
+    full = lax.dynamic_update_slice_in_dim(jnp.zeros(shape, head.dtype), head, here * turn, axis=0)
+    going_up = going_down = head
+    for far in range(1, ways // 2 + 1):
+        going_up = lax.ppermute(going_up, "rows", [(d, (d + 1) % ways) for d in range(ways)])
+        full = lax.dynamic_update_slice_in_dim(full, going_up, (here - far) % ways * turn, axis=0)
+        if 2 * far < ways:
+            going_down = lax.ppermute(
+                going_down, "rows", [(d, (d - 1) % ways) for d in range(ways)]
+            )
+            full = lax.dynamic_update_slice_in_dim(
+                full, going_down, (here + far) % ways * turn, axis=0
+            )
+    panel = full
     vectors, factor = reflect_panel(panel)
     own_vectors = lax.dynamic_slice_in_dim(vectors, rows_place * row_block, row_block, 0)
     partial_cross = jnp.dot(own_vectors.T, gram, precision=lax.Precision.HIGHEST)

time: 2000 us -> 1810 us (0.905)
  local copies, waits for them, and re-layouts: 158 us -> 2.81 us
  starting transfers between devices: 0.38 us -> 39.4 us
  waiting for transfers between devices: 900 us -> 863 us
  other arithmetic: 496 us -> 475 us
    while x512 -> x0, local copies, waits for them, and re-layouts: 156 us -> none
    reduce_sum x64, other arithmetic: 150 us -> 39 us  [one_step(): column = jnp.sum(jnp.where(col_line[None, :] == step, work, 0.0), axis=1)]
    sub x64, other arithmetic: 250 us -> 341 us  [one_step(): work = work - scale * vector[:, None] * project[None, :]]
    all_gather x1 -> x0, waiting for transfers between devices: 64.3 us -> none  [per_device(): panel = lax.all_gather(head, 'rows', axis=0, tiled=True)]
    ppermute x0 -> x15, starting transfers between devices: none -> 39.2 us  [the longest x7 37.5 us: per_device(): lax.ppermute(going_down, 'rows', [(d, (d - 1) % ways) for d in range(ways)])]
    ppermute x0 -> x15, waiting for transfers between devices: none -> 31.4 us  [the longest x8 31.3 us: per_device(): lax.ppermute(going_up, 'rows', [(d, (d + 1) % ways) for d in range(ways)])]
  transfers between devices with their start and end apart: 5 -> 19, of which waited for: 5 -> 13; matrix products, arithmetic and copies ran while one was open for 0% -> 0% of each run, Pallas kernels for 0% -> 0%
where the time goes in v1:
time: 1810 us; the launch traced here: 1800 us
  waiting for transfers between devices  863 us (48%)
  other arithmetic  475 us (26%)
  matrix products  280 us (15%)
  loops' own time  129 us (7%)
  starting transfers between devices  39.4 us (2%)
    reduce_scatter x1, waiting for transfers between devices, per_device(): lax.psum_scatter(product * (col_scale[:, None] * own_scale[None, :] / tot...  685 us
    sub x64, other arithmetic, one_step(): work = work - scale * vector[:, None] * project[None, :]  341 us
    dot_general x64, matrix products, one_step(): coupling = jnp.dot(vector, vectors, precision=lax.Precision.HIGHEST)  174 us
    another operation x1, loops' own time, reflect_panel(): lax.fori_loop(0, width, one_step, (panel, vectors, factor))  129 us
    psum x1, waiting for transfers between devices, per_device(): cross = lax.psum(partial_cross, 'rows')  104 us
    dot_general x64, matrix products, one_step(): project = jnp.dot(vector, work, precision=lax.Precision.HIGHEST)  72.4 us
    reduce_sum x64, other arithmetic, one_step(): length = jnp.sqrt(jnp.sum(column * column))  43.1 us
    reduce_sum x64, other arithmetic, one_step(): scale = 2.0 / jnp.sum(vector * vector)  42.7 us
  transfers between devices with their start and end apart: 19, of which 13 were waited for; matrix products, arithmetic and copies ran while one was open for 0% of the time, Pallas kernels for 0%

profile of v1, /device:TPU:0, one launch (start us, length us, event | category | flops | bytes accessed | tf_op | source)
XLA Modules:
  0.0 1803.3 jit_solution(10774144682287939068)
XLA Ops:
  8.0 17.9 all-gather.2.cloned.1.call-done
  26.0 17.6 multiply_multiply_fusion
  43.6 684.7 %reduce-scatter.2.cloned.1.call-done = f32[256,2048]{1,0:T(8,128)} async-done(((f32[4096,2048]{1,0:T(8,128)}), f32[256,2048]{1,0:T(8,128)}) %reduce-scatter.2.cloned.1.call-update) | async-done | bytes 2097168 | tf_op jit(solution)/shard_map/reduce_scatter | solution.py:57
  730.3 23.9 %all-reduce.3.cloned.1.call-done = f32[256,64]{1,0:T(8,128)} async-done(((f32[256,64]{1,0:T(8,128)}), f32[256,64]{1,0:T(8,128)}) %all-reduce.3.cloned.1.call-update) | async-done | bytes 65552 | tf_op jit(solution)/shard_map/psum | solution.py:11
  764.1 5.5 collective-permute-start.3
  772.6 5.6 collective-permute-start.5
  781.3 5.6 collective-permute-start.7
  790.0 5.6 collective-permute-start.9
  798.5 5.6 collective-permute-start.11
  807.1 5.6 collective-permute-start.13
  816.8 8.5 collective-permute-done.14
  825.3 857.6 %while.19 = (s32[]{:T(128)}, f32[4096,64]{1,0:T(8,128)S(1)}, f32[4096,64]{1,0:T(8,128)}, f32[64,64]{1,0:T(8,128)S(1)}, s32[]{:T(128)}, /*index=5*/f32[]{:T(128)}, f32[]{:T(128)}, f32[]{:T(128)}, f32[]{:T(128)}, s32[]{:T(128)}) while((s32[]{:T(128)}, f32[4096,64]{1,0:T(8,128)S(1)}, f32[4096,64]{1,0:T(8,128)}, ...), condition=%wide.region_7.8_spmd.clone.clone, body=%wide.region_2.7_spmd.clone.clone.sunk | while | flops 8245573 | bytes 7555044 | solution.py:39
  843.7 5.4 multiply_subtract_fusion.2
  857.1 5.4 multiply_subtract_fusion.2
  870.6 5.4 multiply_subtract_fusion.2
  897.5 5.4 multiply_subtract_fusion.2
  964.7 5.4 multiply_subtract_fusion.2
  1018.5 5.4 multiply_subtract_fusion.2
  1031.9 5.4 multiply_subtract_fusion.2
  1085.7 5.4 multiply_subtract_fusion.2
  1153.0 5.4 multiply_subtract_fusion.2
  1220.2 5.4 multiply_subtract_fusion.2
  1274.0 5.4 multiply_subtract_fusion.2
  1287.4 5.4 multiply_subtract_fusion.2
  1341.2 5.4 multiply_subtract_fusion.2
  1408.4 5.4 multiply_subtract_fusion.2
  1475.7 5.4 multiply_subtract_fusion.2
  1529.5 5.4 multiply_subtract_fusion.2
  1542.9 5.4 multiply_subtract_fusion.2
  1596.7 5.4 multiply_subtract_fusion.2
  1663.9 5.4 multiply_subtract_fusion.2
  1687.6 104.3 %all-reduce.5.cloned.1.call-done = f32[64,2048]{1,0:T(8,128)} async-done(((f32[64,2048]{1,0:T(8,128)}), f32[64,2048]{1,0:T(8,128)}) %all-reduce.5.cloned.1.call-update) | async-done | bytes 524304 | tf_op jit(solution)/shard_map/psum | solution.py:83
  (688 shorter events, 668.0 us)
Async XLA Ops:
  7.2 18.8 %copy-start.1 = (bf16[512,2048]{1,0:T(8,128)(2,1)S(1)}, bf16[512,2048]{1,0:T(8,128)(2,1)}, u32[]{:S(2)}) copy-start(bf16[512,2048]{1,0:T(8,128)(2,1)} %param.4) | copy-start | bytes 6291460
  7.2 0.9 copy-start.4
  7.2 18.8 %all-gather.2.cloned.1.call-start = ((), (), s32[]{:S(2)}) async-start(), calls=%async_computation.1 | async-start | bytes 6291456 | tf_op jit(solution)/shard_map/all_gather | solution.py:53
  7.9 720.4 %reduce-scatter.2.cloned.1.call-start = ((), (), s32[]{:S(2)}) async-start(), calls=%async_computation.2 | async-start | bytes 35651584 | tf_op jit(solution)/shard_map/reduce_scatter | solution.py:57
  43.6 710.7 %all-reduce.3.cloned.1.call-start = ((), (), s32[]{:S(2)}) async-start(), calls=%async_computation.3 | async-start | bytes 262144 | tf_op jit(solution)/shard_map/psum | solution.py:11
  729.9 1062.0 %all-reduce.5.cloned.1.call-start = ((), (), s32[]{:S(2)}) async-start(), calls=%async_computation.4 | async-start | bytes 1048576 | tf_op jit(solution)/shard_map/psum | solution.py:83
  754.2 5.8 copy-start.3
  754.2 9.8 collective-permute-start
  756.0 8.2 collective-permute-start.1
  764.0 8.6 collective-permute-start.2
  764.1 8.5 collective-permute-start.3
  772.6 8.7 collective-permute-start.4
  772.6 8.7 collective-permute-start.5
  781.3 8.7 collective-permute-start.6
  781.3 8.7 collective-permute-start.7
  790.0 8.6 collective-permute-start.8
  790.0 8.6 collective-permute-start.9
  798.5 8.6 collective-permute-start.10
  798.5 8.6 collective-permute-start.11
  807.1 9.6 collective-permute-start.12
  807.1 9.7 collective-permute-start.13
  816.8 8.6 collective-permute-start.14
  1683.0 2.4 copy-start
  1685.3 108.2 %copy-start.2 = (f32[256,64]{0,1:T(8,128)}, f32[256,64]{0,1:T(8,128)S(1)}, u32[]{:S(2)}) copy-start(f32[256,64]{0,1:T(8,128)S(1)} %constant_dynamic-slice_fusion) | copy-start | bytes 196612
Sparse Core Ops, SparseCore 0:
  9.6 16.3 all-gather.1
  43.7 684.5 reduce-scatter.1
  730.6 23.5 all-reduce.2
  1687.7 104.1 all-reduce.4
